TPU v7x, 32 devices: a whole 2x2x4 slice. The times are simulated.
32 devices in a mesh: rep: 2 (over y), req: 4 (over z), mp: 4 (over x, core).
Axes of the slice: x: 2, y: 2, z: 4, core: 2. Of those that a mesh axis runs over, the one named last changes fastest.
Arguments:
- hidden_in: bfloat16 [128, 2, 8192], P(('rep', 'req'), None, 'mp'), parts along dimension 0, may hold values from -6 to 6
- frozen_query_rows: bfloat16 [128, 2, 8192], P(('rep', 'req'), None, 'mp'), parts along dimension 0, may hold values from -6 to 86
- new_kv: bfloat16 [128, 2, 2, 1024], P(('rep', 'req'), None, None, 'mp'), parts along dimension 0, may hold values from -6 to 31
- adapter_of: int32 [128], P(('rep', 'req')), parts along dimension 0, may hold values from 0 to 7, as said below
- adapter_home: int32 [16], P('rep'), parts along dimension 0, may hold values from 0 to 7, as said below
- a_store: bfloat16 [16, 64, 8192], P(('rep', 'req'), None, 'mp'), parts along dimension 0, may hold values from -0.0625 to 0.0625
- b_store: bfloat16 [16, 64, 8192], P(('rep', 'req'), None, 'mp'), parts along dimension 0, may hold values from -0.75 to 0.75
- kv_pool: bfloat16 [2, 1024, 16, 1024], P(None, ('rep', 'req'), None, 'mp'), parts along dimension 1, may hold values from -6 to 31
- page_table: int32 [128, 8], P(('rep', 'req')), parts along dimension 0, may hold values from 0 to 127, as said below
- cached_len: int32 [128], P(('rep', 'req')), parts along dimension 0, may hold values from 32 to 128
- new_group: int32 [128], P(('rep', 'req')), parts along dimension 0, may hold values from 0 to 3, as said below
Outputs:
- attended: bfloat16 [128, 2, 8192], P(('rep', 'req'), None, 'mp'), parts along dimension 0
- cache: bfloat16 [2, 128, 128, 1024], P(None, ('rep', 'req'), None, 'mp'), parts along dimension 1
There are 2 independent parts, one for each index of `rep`. A program takes and returns all parts, laid end to end along the dimension named above; each array names one. Nothing has to cross between parts.
Inputs may be any that keep to these rules, and one draw needn't show every extreme that they name: A permutation: adapter a lives in store slot adapter_home[a], which belongs to group adapter_home[a] div 2. `adapter_of`: the requests of one group (new rows h * 16 to h * 16 + 15) use adapters of min(16, number of groups) different owners, at most 4 requests an owner, a number reached in every group; all requests of one group whose adapters have one owner use the same adapter. `page_table`: the rows of one group name each of its 128 pages once. `new_group`: A request keeps its slot (row mod 16); the same 4 slots keep their group in every group; every group receives exactly one request into each slot; no group sends more than 3 requests to one other group, and some pair of groups reaches it.
All inputs are finite; a program needn't handle non-finite values.
Results may differ from a plain program's by a relative error of at most 0.0069.
Values may be sent and summed in bfloat16 or wider, within the bound.
A program may use at most 64 MiB of HBM per device.

v0:
```python
import jax
import jax.numpy as jnp
from jax import lax
from jax.sharding import PartitionSpec as P

HEAD = 128


NEG_FILL = -1e30


def attend(query_vectors, cached_keys, cached_values, length, fresh_kv):
    row_count, step_count, q_width = query_vectors.shape
    context = cached_keys.shape[1]
    kv_width = cached_keys.shape[2]
    kv_heads = kv_width // HEAD
    per_kv = q_width // kv_width
    score_scale = HEAD ** (-0.5)
    q_split = query_vectors.reshape(row_count, step_count, kv_heads, per_kv, HEAD)
    k_split = cached_keys.reshape(row_count, context, kv_heads, HEAD)
    v_split = cached_values.reshape(row_count, context, kv_heads, HEAD)
    new_keys = fresh_kv[:, :, 0].reshape(row_count, step_count, kv_heads, HEAD)
    new_values = fresh_kv[:, :, 1].reshape(row_count, step_count, kv_heads, HEAD)
    old_scores = (
        jnp.einsum("bskgd,bjkd->bskgj", q_split, k_split, preferred_element_type=jnp.float32)
        * score_scale
    )
    visible = jnp.arange(context)[None, :] < length[:, None]
    old_scores = jnp.where(visible[:, None, None, None, :], old_scores, NEG_FILL)
    new_scores = (
        jnp.einsum("bskgd,btkd->bskgt", q_split, new_keys, preferred_element_type=jnp.float32)
        * score_scale
    )
    causal = jnp.arange(step_count)[None, :] <= jnp.arange(step_count)[:, None]
    new_scores = jnp.where(causal[None, :, None, None, :], new_scores, NEG_FILL)
    scores = jnp.concatenate([old_scores, new_scores], axis=-1)
    row_max = jnp.max(scores, axis=-1, keepdims=True)
    weights = jnp.exp(scores - row_max)
    probabilities = (weights / jnp.sum(weights, axis=-1, keepdims=True)).astype(jnp.bfloat16)
    attention_out = jnp.einsum(
        "bskgj,bjkd->bskgd",
        probabilities[..., :context],
        v_split,
        preferred_element_type=jnp.float32,
    )
    attention_out = attention_out + jnp.einsum(
        "bskgt,btkd->bskgd",
        probabilities[..., context:],
        new_values,
        preferred_element_type=jnp.float32,
    )
    return attention_out.reshape(row_count, step_count, q_width).astype(jnp.bfloat16)


def adapter_rank_width(rank_partial_sum):
    return lax.psum(rank_partial_sum, "mp")


def per_device(
    hidden_in,
    frozen_query_rows,
    new_kv,
    adapter_of,
    adapter_home,
    a_store,
    b_store,
    kv_pool,
    page_table,
    cached_len,
    new_group,
):
    groups = lax.axis_size("req")
    my_group = lax.axis_index("req")
    per_group = adapter_of.shape[0]
    store_count = a_store.shape[0]
    context = page_table.shape[1] * kv_pool.shape[2]
    kv_width = kv_pool.shape[3]
    move_cap = -(-(per_group - per_group // 4) // groups)
    group_ids = jnp.arange(groups, dtype=jnp.int32)
    slot_ids = jnp.arange(per_group, dtype=jnp.int32)
    buffer_ids = jnp.arange(groups * move_cap, dtype=jnp.int32)
    adapter_slot = jnp.take(adapter_home, adapter_of)
    owners = adapter_slot // store_count
    local_pick = adapter_slot % store_count
    owner_hit = owners[:, None] == group_ids[None, :]
    wanted = jnp.max(jnp.where(owner_hit, local_pick[:, None], -1), axis=0)
    moving = new_group != my_group
    dest_hit = (new_group[:, None] == group_ids[None, :]) & moving[:, None]
    order_in = jnp.cumsum(dest_hit.astype(jnp.int32), axis=0) - 1
    position = jnp.sum(jnp.where(dest_hit, order_in, 0), axis=1)
    flat_slot = jnp.where(moving, new_group * move_cap + position, -1)
    slot_match = flat_slot[None, :] == buffer_ids[:, None]
    send_src = jnp.where(
        jnp.any(slot_match, axis=1),
        jnp.sum(jnp.where(slot_match, slot_ids[None, :], 0), axis=1),
        -1,
    )
    safe_src = jnp.maximum(send_src, 0)
    send_len = jnp.where(send_src >= 0, jnp.take(cached_len, safe_src), 0)
    got_wanted, got_slots, got_lens = (
        lax.all_to_all(wanted, "req", split_axis=0, concat_axis=0, tiled=True),
        lax.all_to_all(
            send_src.reshape(groups, move_cap), "req", split_axis=0, concat_axis=0, tiled=True
        ),
        lax.all_to_all(
            send_len.reshape(groups, move_cap), "req", split_axis=0, concat_axis=0, tiled=True
        ),
    )
    page_rows = jnp.take(kv_pool, page_table.reshape(-1), axis=1)
    cache_old = page_rows.reshape(2, per_group, context, kv_width)
    incoming = got_slots.reshape(-1)
    in_match = incoming[None, :] == slot_ids[:, None]
    in_index = jnp.sum(jnp.where(in_match, buffer_ids[None, :], 0), axis=1)
    len_new = jnp.where(moving, jnp.take(got_lens.reshape(-1), in_index), cached_len)
    wanted_slot = jnp.maximum(got_wanted, 0)
    a_panels, b_panels = (
        lax.all_to_all(
            jnp.take(a_store, wanted_slot, axis=0), "req", split_axis=0, concat_axis=0, tiled=True
        ),
        lax.all_to_all(
            jnp.take(b_store, wanted_slot, axis=0), "req", split_axis=0, concat_axis=0, tiled=True
        ),
    )
    a_rows = jnp.take(a_panels, owners, axis=0)
    up_panel_rows = jnp.take(b_panels, owners, axis=0)
    rank_slice_product = jnp.einsum(
        "rsd,rkd->rsk", hidden_in, a_rows, preferred_element_type=jnp.float32
    )
    complete_rank_product = adapter_rank_width(rank_slice_product).astype(jnp.bfloat16)
    adapter_query_delta = jnp.einsum(
        "gxj,gjv->gxv", complete_rank_product, up_panel_rows, preferred_element_type=jnp.float32
    )
    query_vectors = (frozen_query_rows.astype(jnp.float32) + adapter_query_delta).astype(
        jnp.bfloat16
    )
    far_cache = jnp.take(cache_old, safe_src, axis=1)
    send_pages = far_cache.reshape(2, groups, move_cap, context, kv_width)
    got_pages = lax.all_to_all(send_pages, "req", split_axis=1, concat_axis=1, tiled=True)
    pooled = jnp.concatenate(
        [cache_old, got_pages.reshape(2, groups * move_cap, context, kv_width)], axis=1
    )
    source = jnp.where(moving, per_group + in_index, slot_ids)
    cache_new = jnp.take(pooled, source, axis=1)
    attended = attend(query_vectors, cache_new[0], cache_new[1], len_new, new_kv)
    return (attended, cache_new)


def solution(mesh):
    placed = (
        P(("rep", "req"), None, "mp"),
        P(("rep", "req"), None, "mp"),
        P(("rep", "req"), None, None, "mp"),
        P(("rep", "req")),
        P("rep"),
        P(("rep", "req"), None, "mp"),
        P(("rep", "req"), None, "mp"),
        P(None, ("rep", "req"), None, "mp"),
        P(("rep", "req"), None),
        P(("rep", "req")),
        P(("rep", "req")),
    )
    return jax.shard_map(
        per_device,
        mesh=mesh,
        in_specs=placed,
        out_specs=(P(("rep", "req"), None, "mp"), P(None, ("rep", "req"), None, "mp")),
        check_vma=False,
    )
```

profile of v0, /device:TPU:0, one launch (start us, length us, event | category | flops | bytes accessed | tf_op | source)
XLA Modules:
  0.0 155.8 jit_solution(11224241576532435948)
XLA Ops:
  0.6 0.8 compare_select_fusion.3
  1.5 1.3 gather_fusion.5
  2.8 0.7 compare_and_fusion.1
  3.6 0.7 copy.112
  4.2 6.3 %all-to-all-start.3 = ((s32[4,1,1]{2,1,0:T(1,128)}), s32[4,1,1]{2,1,0:T(1,128)S(1)}, u32[]{:S(2)}, u32[]{:S(2)}) async-start(s32[4,1,1]{2,1,0:T(1,128)} %copy.112), calls=%async_computation.3 | async-start | bytes 4096 | tf_op jit(solution)/shard_map/all_to_all | solution.py:101
  11.2 0.7 fusion.34
  12.0 0.8 select_reduce_fusion.3
  12.8 0.7 add_select_fusion
  13.7 0.7 select_n.200
  14.4 1.3 gather_fusion.3
  15.8 1.3 select_select_fusion
  17.1 5.1 %all-to-all-start = ((s32[4,1,3]{2,1,0:T(1,128)}), s32[4,1,3]{2,1,0:T(1,128)S(1)}, u32[]{:S(2)}, u32[]{:S(2)}) async-start(s32[4,1,3]{2,1,0:T(1,128)} %bitcast), calls=%async_computation | async-start | bytes 4096 | tf_op jit(solution)/shard_map/all_to_all | solution.py:102
  22.4 1.7 %gather_fusion.6 = bf16[4,64,2048]{2,1,0:T(8,128)(2,1)S(1)} fusion(bf16[2,64,2048]{2,1,0:T(8,128)(2,1)} %param.20, s32[1024]{0:T(1024)S(1)} %pad_clamp_fusion.1), kind=kCustom, calls=%fused_computation.clone | custom fusion | bytes 2097168 | tf_op jit(solution)/shard_map/jit(_take)/gather | solution.py:118
  24.0 2.6 %gather_fusion.8 = bf16[4,64,2048]{2,1,0:T(8,128)(2,1)} fusion(bf16[2,64,2048]{2,1,0:T(8,128)(2,1)} %param.21, s32[1024]{0:T(1024)S(1)} %pad_clamp_fusion.1), kind=kCustom, calls=%fused_computation.2.clone | custom fusion | bytes 2097168 | tf_op jit(solution)/shard_map/jit(_take)/gather | solution.py:121
  26.7 1.0 all-to-all-done
  27.6 4.1 %all-to-all-start.2 = ((s32[4,1,3]{2,1,0:T(1,128)}), s32[4,1,3]{2,1,0:T(1,128)S(1)}, u32[]{:S(2)}, u32[]{:S(2)}) async-start(s32[4,1,3]{2,1,0:T(1,128)} %bitcast.10), calls=%async_computation.2 | async-start | bytes 4096 | tf_op jit(solution)/shard_map/all_to_all | solution.py:105
  31.8 2.8 %broadcast_select_fusion.1 = (bf16[4,64,2048]{2,1,0:T(8,128)(2,1)}, bf16[4,64,2048]{2,1,0:T(8,128)(2,1)}) fusion(bf16[4,64,2048]{2,1,0:T(8,128)(2,1)S(1)} %gather_fusion.6, pred[4]{0:T(512)(128)(4,1)S(1)} %compare_and_fusion.2, bf16[4,64,2048]{2,1,0:T(8,128)(2,1)} %gather_fusion.8), kind=kLoop, calls=%fused_computation.36 | loop fusion | flops 1048576 | bytes 4194308 | tf_op jit(solution)/shard_map/jit(_take)/select_n | solution.py:118
  34.6 2.6 %all-to-all-done.2 = s32[4,1,3]{2,1,0:T(1,128)S(1)} async-done(((s32[4,1,3]{2,1,0:T(1,128)}), s32[4,1,3]{2,1,0:T(1,128)S(1)}, u32[]{:S(2)}, u32[]{:S(2)}) %all-to-all-start.2) | async-done | bytes 80 | tf_op jit(solution)/shard_map/all_to_all | solution.py:105
  37.1 3.5 %all-to-all-start.4 = ((bf16[4,64,2048]{2,1,0:T(8,128)(2,1)}), bf16[4,64,2048]{2,1,0:T(8,128)(2,1)S(1)}, u32[]{:S(2)}, u32[]{:S(2)}) async-start(bf16[4,64,2048]{2,1,0:T(8,128)(2,1)} %get-tuple-element.25), calls=%async_computation.4 | async-start | bytes 2097152 | tf_op jit(solution)/shard_map/all_to_all | solution.py:117
  40.8 23.4 %all-to-all-done.4 = bf16[4,64,2048]{2,1,0:T(8,128)(2,1)S(1)} async-done(((bf16[4,64,2048]{2,1,0:T(8,128)(2,1)}), bf16[4,64,2048]{2,1,0:T(8,128)(2,1)S(1)}, u32[]{:S(2)}, u32[]{:S(2)}) %all-to-all-start.4) | async-done | bytes 1048608 | tf_op jit(solution)/shard_map/all_to_all | solution.py:117
  64.2 4.2 %all-to-all-start.5 = ((bf16[4,64,2048]{2,1,0:T(8,128)(2,1)}), bf16[4,64,2048]{2,1,0:T(8,128)(2,1)}, u32[]{:S(2)}, u32[]{:S(2)}) async-start(bf16[4,64,2048]{2,1,0:T(8,128)(2,1)} %get-tuple-element.26), calls=%async_computation.5 | async-start | bytes 2097152 | tf_op jit(solution)/shard_map/all_to_all | solution.py:120
  68.5 2.0 %gather_fusion = bf16[128,2,16,256]{3,2,1,0:T(8,128)(2,1)} fusion(bf16[2,128,16,256]{3,2,1,0:T(8,128)(2,1)S(1)} %copy-done, s32[1024]{0:T(1024)S(1)} %pad_clamp_fusion.6), kind=kCustom, calls=%fused_computation.4 | custom fusion | bytes 4194816 | tf_op jit(solution)/shard_map/jit(_take)/gather | solution.py:109
  70.5 3.1 %copy.106 = bf16[2,128,16,256]{3,2,1,0:T(8,128)(2,1)} copy(bf16[2,128,16,256]{3,2,0,1:T(8,128)(2,1)} %bitcast.52) | data formatting | bytes 4194304 | tf_op jit(solution)/shard_map/jit(_take)/gather | solution.py:109
  73.9 2.8 %bitcast_select_fusion = bf16[2,16,128,256]{3,2,1,0:T(8,128)(2,1)} fusion(pred[16,128]{1,0:T(8,128)(4,1)S(1)} %broadcast_in_dim.159, bf16[2,16,128,256]{3,2,1,0:T(8,128)(2,1)} %bitcast.51), kind=kLoop, calls=%fused_computation.19 | loop fusion | flops 1048576 | bytes 4196352 | tf_op jit(solution)/shard_map/jit(_take)/select_n | solution.py:109
  76.7 3.4 %gather_fusion.1 = bf16[12,2,128,256]{3,2,1,0:T(8,128)(2,1)} fusion(bf16[2,16,128,256]{3,2,1,0:T(8,128)(2,1)} %bitcast_select_fusion, s32[1024]{0:T(1024)S(1)} %pad_clamp_fusion.5), kind=kCustom, calls=%fused_computation.5 | custom fusion | bytes 3145776 | tf_op jit(solution)/shard_map/jit(_take)/gather | solution.py:136
  81.0 2.9 %copy_select_fusion = bf16[2,4,3,128,256]{4,3,2,0,1:T(8,128)(2,1)} fusion(bf16[2,4,3,128,256]{4,3,0,2,1:T(8,128)(2,1)} %bitcast.54, pred[4,3]{1,0:T(4,128)(4,1)S(1)} %le.81), kind=kLoop, calls=%fused_computation.23 | loop fusion | flops 786432 | bytes 3145740 | tf_op jit(solution)/shard_map/jit(_take)/select_n | solution.py:136
  83.9 9.9 %all-to-all-done.5 = bf16[4,64,2048]{2,1,0:T(8,128)(2,1)} async-done(((bf16[4,64,2048]{2,1,0:T(8,128)(2,1)}), bf16[4,64,2048]{2,1,0:T(8,128)(2,1)}, u32[]{:S(2)}, u32[]{:S(2)}) %all-to-all-start.5) | async-done | bytes 1048608 | tf_op jit(solution)/shard_map/all_to_all | solution.py:120
  93.8 4.3 %all-to-all-start.1 = ((bf16[2,4,3,128,256]{4,3,2,0,1:T(8,128)(2,1)}), bf16[2,4,3,128,256]{4,3,2,0,1:T(8,128)(2,1)}, u32[]{:S(2)}, u32[]{:S(2)}) async-start(bf16[2,4,3,128,256]{4,3,2,0,1:T(8,128)(2,1)} %copy_select_fusion), calls=%async_computation.1 | async-start | bytes 3145728 | tf_op jit(solution)/shard_map/all_to_all | solution.py:138
  102.7 0.7 iota_compare_fusion.1
  103.3 2.8 %gather_fusion.7 = bf16[16,64,2048]{2,1,0:T(8,128)(2,1)} fusion(bf16[4,64,2048]{2,1,0:T(8,128)(2,1)S(1)} %all-to-all-done.4, s32[1024]{0:T(1024)S(1)} %pad_clamp_fusion), kind=kCustom, calls=%fused_computation.1.clone | custom fusion | bytes 8388672 | tf_op jit(solution)/shard_map/jit(_take)/gather | solution.py:124
  106.1 4.0 %gather_fusion.9 = bf16[16,64,2048]{2,1,0:T(8,128)(2,1)} fusion(bf16[4,64,2048]{2,1,0:T(8,128)(2,1)} %all-to-all-done.5, s32[1024]{0:T(1024)S(1)} %pad_clamp_fusion), kind=kCustom, calls=%fused_computation.3.clone | custom fusion | bytes 8388672 | tf_op jit(solution)/shard_map/jit(_take)/gather | solution.py:125
  110.1 3.5 %fusion.20 = f32[16,2,64]{2,1,0:T(2,128)S(1)} fusion(bf16[16,2,2048]{2,1,0:T(2,128)(2,1)S(1)} %copy-done.9, bf16[16,64,2048]{2,1,0:T(8,128)(2,1)} %gather_fusion.7, pred[16]{0:T(512)(128)(4,1)S(1)} %get-tuple-element.16), kind=kOutput, calls=%fused_computation.34 | convolution fusion | flops 10485760 | bytes 4333584 | tf_op jit(solution)/shard_map/rsd,rkd->rsk/dot_general | solution.py:126
  113.6 10.2 %psum.7 = bf16[16,2,64]{2,1,0:T(2,128)(2,1)S(1)} all-reduce(f32[16,2,64]{2,1,0:T(2,128)S(1)} %fusion.20), channel_id=1, replica_groups=mesh['rep'=2,'req'=4,'mp'=4] {'mp'}, use_global_device_ids=true, to_apply=%region_6.9 | all-reduce | flops 2048 | bytes 12288 | tf_op jit(solution)/shard_map/psum | solution.py:56
  123.8 2.9 %fusion.9 = bf16[16,2,2048]{2,1,0:T(2,128)(2,1)S(1)} fusion(bf16[16,64,2048]{2,1,0:T(8,128)(2,1)} %gather_fusion.9, pred[16]{0:T(512)(128)(4,1)S(1)} %get-tuple-element.16, bf16[16,2,2048]{2,1,0:T(2,128)(2,1)S(1)} %copy-done.10, bf16[16,2,64]{2,1,0:T(2,128)(2,1)S(1)} %psum.7), kind=kOutput, calls=%fused_computation.18 | convolution fusion | flops 10682368 | bytes 4460560 | tf_op jit(solution)/shard_map/gxj,gjv->gxv/dot_general | solution.py:130
  126.9 0.9 fusion.42
  127.8 6.8 %all-to-all-done.1 = bf16[2,4,3,128,256]{4,3,2,0,1:T(8,128)(2,1)} async-done(((bf16[2,4,3,128,256]{4,3,2,0,1:T(8,128)(2,1)}), bf16[2,4,3,128,256]{4,3,2,0,1:T(8,128)(2,1)}, u32[]{:S(2)}, u32[]{:S(2)}) %all-to-all-start.1) | async-done | bytes 1572896 | tf_op jit(solution)/shard_map/all_to_all | solution.py:138
  134.6 1.7 %copy.108 = bf16[2,4,3,128,256]{4,3,2,1,0:T(8,128)(2,1)S(1)} copy(bf16[2,4,3,128,256]{4,3,2,0,1:T(8,128)(2,1)} %all-to-all-done.1) | data formatting | bytes 3145728 | tf_op jit(solution)/shard_map/all_to_all | solution.py:138
  136.7 2.1 %pad_maximum_fusion = bf16[2,28,128,256]{3,2,1,0:T(8,128)(2,1)} fusion(bf16[2,12,128,256]{3,2,1,0:T(8,128)(2,1)S(1)} %bitcast.53, bf16[2,16,128,256]{3,2,1,0:T(8,128)(2,1)S(1)} %copy-done.2), kind=kLoop, calls=%fused_computation.16 | loop fusion | flops 1835008 | bytes 7340032 | tf_op jit(solution)/shard_map/concatenate | solution.py:139
  138.8 4.2 %gather_fusion.2 = bf16[16,2,128,256]{3,2,1,0:T(8,128)(2,1)} fusion(bf16[2,28,128,256]{3,2,1,0:T(8,128)(2,1)} %pad_maximum_fusion, s32[1024]{0:T(1024)} %pad_clamp_fusion.4), kind=kCustom, calls=%fused_computation.6 | custom fusion | bytes 4194368 | tf_op jit(solution)/shard_map/jit(_take)/gather | solution.py:143
  143.0 1.9 %select_bitcast_fusion = bf16[2,16,128,256]{3,2,0,1:T(8,128)(2,1)S(1)} fusion(bf16[16,2,128,256]{3,2,1,0:T(8,128)(2,1)} %gather_fusion.2, pred[16]{0:T(512)(128)(4,1)S(1)} %copy-done.8), kind=kLoop, calls=%fused_computation.22 | loop fusion | flops 1048576 | bytes 4194320 | tf_op jit(solution)/shard_map/jit(_take)/select_n | solution.py:143
  144.8 1.5 fusion.40
  146.3 1.5 copy.125
  147.8 1.6 %copy.111 = bf16[1,16,128,256]{2,3,1,0:T(8,128)(2,1)S(1)} copy(bf16[1,16,128,256]{3,2,0,1:T(8,128)(2,1)} %get-tuple-element.23) | data formatting | bytes 2097152 | tf_op jit(solution)/shard_map/slice | solution.py:144
  149.4 1.2 fusion.41
  150.6 0.8 reduce_max.32
  151.7 0.9 divide_convert_fusion
  152.6 1.7 %copy.109 = bf16[1,16,128,256]{2,3,1,0:T(8,128)(2,1)S(1)} copy(bf16[1,16,128,256]{3,2,0,1:T(8,128)(2,1)} %get-tuple-element.24) | data formatting | bytes 2097152 | tf_op jit(solution)/shard_map/slice | solution.py:144
  155.1 0.7 reshape.372
  (72 shorter events, 8.8 us)
Async XLA Ops:
  0.6 67.9 %copy-start = (bf16[2,128,16,256]{3,2,1,0:T(8,128)(2,1)S(1)}, bf16[2,128,16,256]{3,2,1,0:T(8,128)(2,1)}, u32[]{:S(2)}) copy-start(bf16[2,128,16,256]{3,2,1,0:T(8,128)(2,1)} %param.22) | copy-start | bytes 6291460
  4.2 12.9 %all-to-all-start.3 = ((s32[4,1,1]{2,1,0:T(1,128)}), s32[4,1,1]{2,1,0:T(1,128)S(1)}, u32[]{:S(2)}, u32[]{:S(2)}) async-start(s32[4,1,1]{2,1,0:T(1,128)} %copy.112), calls=%async_computation.3 | async-start | bytes 4096 | tf_op jit(solution)/shard_map/all_to_all | solution.py:101
  17.1 10.6 %all-to-all-start = ((s32[4,1,3]{2,1,0:T(1,128)}), s32[4,1,3]{2,1,0:T(1,128)S(1)}, u32[]{:S(2)}, u32[]{:S(2)}) async-start(s32[4,1,3]{2,1,0:T(1,128)} %bitcast), calls=%async_computation | async-start | bytes 4096 | tf_op jit(solution)/shard_map/all_to_all | solution.py:102
  27.6 9.5 %all-to-all-start.2 = ((s32[4,1,3]{2,1,0:T(1,128)}), s32[4,1,3]{2,1,0:T(1,128)S(1)}, u32[]{:S(2)}, u32[]{:S(2)}) async-start(s32[4,1,3]{2,1,0:T(1,128)} %bitcast.10), calls=%async_computation.2 | async-start | bytes 4096 | tf_op jit(solution)/shard_map/all_to_all | solution.py:105
  34.6 6.1 %copy-start.5 = (s32[16,8]{0,1:T(8,128)S(1)}, s32[16,8]{0,1:T(8,128)}, u32[]{:S(2)}) copy-start(s32[16,8]{0,1:T(8,128)} %param.23) | copy-start | bytes 1540
  37.1 27.1 %all-to-all-start.4 = ((bf16[4,64,2048]{2,1,0:T(8,128)(2,1)}), bf16[4,64,2048]{2,1,0:T(8,128)(2,1)S(1)}, u32[]{:S(2)}, u32[]{:S(2)}) async-start(bf16[4,64,2048]{2,1,0:T(8,128)(2,1)} %get-tuple-element.25), calls=%async_computation.4 | async-start | bytes 2097152 | tf_op jit(solution)/shard_map/all_to_all | solution.py:117
  64.2 29.5 %all-to-all-start.5 = ((bf16[4,64,2048]{2,1,0:T(8,128)(2,1)}), bf16[4,64,2048]{2,1,0:T(8,128)(2,1)}, u32[]{:S(2)}, u32[]{:S(2)}) async-start(bf16[4,64,2048]{2,1,0:T(8,128)(2,1)} %get-tuple-element.26), calls=%async_computation.5 | async-start | bytes 2097152 | tf_op jit(solution)/shard_map/all_to_all | solution.py:120
  76.7 3.5 %copy-start.4 = (bf16[16,2,2,256]{3,2,1,0:T(2,128)(2,1)S(1)}, bf16[16,2,2,256]{3,2,1,0:T(2,128)(2,1)}, u32[]{:S(2)}) copy-start(bf16[16,2,2,256]{3,2,1,0:T(2,128)(2,1)} %param.17) | copy-start | bytes 98308
  83.9 17.6 %copy-start.7 = (s32[16]{0:T(128)S(1)}, s32[16]{0:T(128)}, u32[]{:S(2)}) copy-start(s32[16]{0:T(128)} %param.25) | copy-start | bytes 196
  83.9 18.8 %copy-start.1 = (s32[16]{0:T(128)S(1)}, s32[16]{0:T(128)}, u32[]{:S(2)}) copy-start(s32[16]{0:T(128)} %param.24) | copy-start | bytes 196
  93.8 40.9 %all-to-all-start.1 = ((bf16[2,4,3,128,256]{4,3,2,0,1:T(8,128)(2,1)}), bf16[2,4,3,128,256]{4,3,2,0,1:T(8,128)(2,1)}, u32[]{:S(2)}, u32[]{:S(2)}) async-start(bf16[2,4,3,128,256]{4,3,2,0,1:T(8,128)(2,1)} %copy_select_fusion), calls=%async_computation.1 | async-start | bytes 3145728 | tf_op jit(solution)/shard_map/all_to_all | solution.py:138
  106.1 4.0 %copy-start.9 = (bf16[16,2,2048]{2,1,0:T(2,128)(2,1)S(1)}, bf16[16,2,2048]{2,1,0:T(2,128)(2,1)}, u32[]{:S(2)}) copy-start(bf16[16,2,2048]{2,1,0:T(2,128)(2,1)} %param.15) | copy-start | bytes 393220
  110.1 13.7 %copy-start.10 = (bf16[16,2,2048]{2,1,0:T(2,128)(2,1)S(1)}, bf16[16,2,2048]{2,1,0:T(2,128)(2,1)}, u32[]{:S(2)}) copy-start(bf16[16,2,2048]{2,1,0:T(2,128)(2,1)} %param.16) | copy-start | bytes 393220
  123.8 3.1 %copy-start.6 = (bf16[16,2,2,128]{3,2,1,0:T(2,128)(2,1)S(1)}, bf16[16,2,2,128]{3,2,1,0:T(2,128)(2,1)}, u32[]{:S(2)}) copy-start(bf16[16,2,2,128]{3,2,1,0:T(2,128)(2,1)} %reshape.370) | copy-start | bytes 49156
  123.8 3.1 %copy-start.11 = (pred[2,2]{1,0:T(4,128)(4,1)S(1)}, pred[2,2]{1,0:T(4,128)(4,1)}, u32[]{:S(2)}) copy-start(pred[2,2]{1,0:T(4,128)(4,1)} %iota_compare_fusion.5) | copy-start | bytes 16
  134.6 2.1 %copy-start.2 = (bf16[2,16,128,256]{3,2,1,0:T(8,128)(2,1)S(1)}, bf16[2,16,128,256]{3,2,1,0:T(8,128)(2,1)}, u32[]{:S(2)}) copy-start(bf16[2,16,128,256]{3,2,1,0:T(8,128)(2,1)} %bitcast_select_fusion) | copy-start | bytes 6291460
  138.8 4.2 %copy-start.8 = (pred[16]{0:T(512)(128)(4,1)S(1)}, pred[16]{0:T(512)(128)(4,1)}, u32[]{:S(2)}) copy-start(pred[16]{0:T(512)(128)(4,1)} %get-tuple-element.19) | copy-start | bytes 52
  152.6 1.7 %copy-start.3 = (bf16[16,2,2,8,130]{4,3,1,2,0:T(8,128)(2,1)S(1)}, bf16[16,2,2,8,130]{4,3,1,2,0:T(8,128)(2,1)}, u32[]{:S(2)}) copy-start(bf16[16,2,2,8,130]{4,3,1,2,0:T(8,128)(2,1)} %divide_convert_fusion) | copy-start | bytes 399364
where the time goes:
time: 157 us; the launch traced here: 156 us
  waiting for transfers between devices  43.7 us (28%)
  local copies, waits for them, and re-layouts  39.6 us (25%)
  starting transfers between devices  27.6 us (18%)
  other arithmetic  24.5 us (16%)
  blocking collectives  10.2 us (6%)
  matrix products  9.32 us (6%)
    all_to_all x1, waiting for transfers between devices, per_device(): lax.all_to_all(jnp.take(a_store, wanted_slot, axis=0), 'req', split_axis=...  23.4 us
    psum x1, blocking collectives, adapter_rank_width(): return lax.psum(rank_partial_sum, 'mp')  10.2 us
    all_to_all x1, waiting for transfers between devices, per_device(): lax.all_to_all(jnp.take(b_store, wanted_slot, axis=0), 'req', split_axis=...  9.87 us
    all_to_all x1, waiting for transfers between devices, per_device(): lax.all_to_all(send_pages, 'req', split_axis=1, concat_axis=1, tiled=True)  6.84 us
    all_to_all x1, starting transfers between devices, per_device(): lax.all_to_all(wanted, 'req', split_axis=0, concat_axis=0, tiled=True)  6.32 us
    gather x2, local copies, waits for them, and re-layouts, per_device(): page_rows = jnp.take(kv_pool, page_table.reshape(-1), axis=1)  5.1 us
    all_to_all x1, starting transfers between devices, per_device(): lax.all_to_all(send_src.reshape(groups, move_cap), 'req', split_axis=0, c...  5.09 us
    all_to_all x1, starting transfers between devices, per_device(): lax.all_to_all(send_pages, 'req', split_axis=1, concat_axis=1, tiled=True)  4.35 us
  transfers between devices with their start and end apart: 6, of which 5 were waited for; matrix products, arithmetic and copies ran while one was open for 31% of the time, Pallas kernels for 0%

commit v1 on v0

v1 whole, which is shorter than its diff:
```python
import functools

import jax
import jax.numpy as jnp
from jax import lax
from jax.experimental import pallas as pl
from jax.experimental.pallas import tpu as pltpu
from jax.sharding import PartitionSpec as P

HEAD = 128
NEG_FILL = -1e30
MESH = pl.DeviceIdType.MESH
VMEM = pltpu.VMEM
SMEM = pltpu.SMEM


def kernel(
    cfg,
    adapter_of,
    adapter_home,
    page_table,
    cached_len,
    new_group,
    hidden,
    frozen,
    fresh,
    a_panels,
    b_panels,
    pool,
    att_out,
    cache_out,
    h_send,
    h_all,
    f_send,
    f_all,
    r_part,
    r_all,
    q_send,
    q_all,
    q_rows,
    meta_send,
    meta_all,
    meta_s,
    page_send,
    rows,
    att,
    h_ss,
    h_rs,
    f_ss,
    f_rs,
    r_ss,
    r_rs,
    q_ss,
    q_rs,
    m_ss,
    m_rs,
    p_ss,
    p_rs,
    l_sem,
):
    groups, mps, per_group, steps, cap, block, store_count, rank, pages, page, move_cap = cfg
    f32, bf16 = jnp.float32, jnp.bfloat16
    rep = lax.axis_index("rep")
    me = lax.axis_index("req")
    mp = lax.axis_index("mp")
    width = hidden.shape[1]
    lanes = store_count * rank
    kv_width = pool.shape[3]
    kv_heads = kv_width // HEAD
    per_kv = width // kv_width
    context = pages * page
    sent_rows = groups * block
    own_rows = per_group * steps

    def peer(d):
        return lax.rem(me + d, groups)

    def send_to(d):
        return (rep, peer(d), mp)

    barrier = pltpu.get_barrier_semaphore()
    for d in range(1, groups):
        pl.semaphore_signal(barrier, inc=1, device_id=send_to(d), device_id_type=MESH)
    for d in range(1, mps):
        pl.semaphore_signal(
            barrier, inc=1, device_id=(rep, me, lax.rem(mp + d, mps)), device_id_type=MESH
        )

    owners, picks, targets = [], [], []
    for r in range(per_group):
        home = adapter_home[adapter_of[r]]
        owner = home // store_count
        picks.append(home - owner * store_count)
        place = jnp.int32(0)
        for o in owners:
            place = place + (o == owner).astype(jnp.int32)
        owners.append(owner)
        targets.append(owner * block + place * steps)
    col = lax.broadcasted_iota(jnp.int32, (sent_rows, own_rows), 1)
    row = lax.broadcasted_iota(jnp.int32, (sent_rows, own_rows), 0)
    want = jnp.zeros((sent_rows, own_rows), jnp.int32)
    mrow = lax.broadcasted_iota(jnp.int32, (own_rows, lanes), 0) // steps
    mlane = lax.broadcasted_iota(jnp.int32, (own_rows, lanes), 1) // rank
    mpick = jnp.zeros((own_rows, lanes), jnp.int32)
    for r in range(per_group):
        want = jnp.where(col // steps == r, targets[r] + lax.rem(col, steps), want)
        mpick = jnp.where(mrow == r, picks[r], mpick)
    pick_by_owner = (row == want).astype(f32).astype(bf16)
    mask = (mlane == mpick).astype(f32).astype(bf16)

    h_out = jnp.dot(pick_by_owner, hidden[...], preferred_element_type=f32)
    m_out = jnp.dot(pick_by_owner, mask, preferred_element_type=f32)
    h_send[:, :, :width] = h_out.reshape(groups, block, width).astype(bf16)
    h_send[:, :, width:] = m_out.reshape(groups, block, lanes).astype(bf16)
    mi = lax.broadcasted_iota(jnp.int32, (8, 128), 0)
    mj = lax.broadcasted_iota(jnp.int32, (8, 128), 1)
    meta = jnp.zeros((8, 128), jnp.int32)
    for r in range(per_group):
        meta = jnp.where((mi == 0) & (mj == r), new_group[r], meta)
        meta = jnp.where((mi == 1) & (mj == r), cached_len[r], meta)
    meta_send[...] = meta

    pl.semaphore_wait(barrier, groups - 1 + mps - 1)

    def copies(src, dst, ss, rs):
        out = {}
        for d in range(1, groups):
            out[d] = pltpu.make_async_remote_copy(
                src_ref=src(d),
                dst_ref=dst,
                send_sem=ss.at[d - 1],
                recv_sem=rs.at[d - 1],
                device_id=send_to(d),
                device_id_type=MESH,
            )
        return out

    h_cp = copies(lambda d: h_send.at[peer(d)], h_all.at[me], h_ss, h_rs)
    order = sorted(range(1, groups), key=lambda d: -min(d, groups - d))
    for d in order:
        h_cp[d].start()
    h_all[me] = h_send[me]

    f_out = jnp.dot(pick_by_owner, frozen[...], preferred_element_type=f32)
    f_send[...] = f_out.reshape(groups, block, width).astype(bf16)
    f_cp = copies(lambda d: f_send.at[peer(d)], f_all.at[me], f_ss, f_rs)
    for d in order:
        f_cp[d].start()
    f_all[me] = f_send[me]
    m_cp = copies(lambda d: meta_send, meta_all.at[me], m_ss, m_rs)
    for d in order:
        m_cp[d].start()
    meta_all[me] = meta

    p_cp = {}
    for d in order:
        dest = peer(d)
        count = jnp.int32(0)
        sources = [jnp.int32(0)] * move_cap
        for r in range(per_group):
            hit = new_group[r] == dest
            for k in range(move_cap):
                sources[k] = jnp.where(hit & (count == k), r, sources[k])
            count = count + hit.astype(jnp.int32)
        for k in range(move_cap):
            slot = (d - 1) * move_cap + k
            for j in range(pages):
                page_id = page_table[sources[k] * pages + j]
                page_send[slot, :, pl.ds(j * page, page), :] = pool[:, page_id]
            p_cp[slot] = pltpu.make_async_remote_copy(
                src_ref=page_send.at[slot],
                dst_ref=rows.at[per_group + slot],
                send_sem=p_ss.at[slot],
                recv_sem=p_rs.at[slot],
                device_id=send_to(d),
                device_id_type=MESH,
            )
            p_cp[slot].start()

    for d in range(1, groups):
        h_cp[d].wait_recv()
    h_in = h_all[...].astype(f32).reshape(sent_rows, width + lanes)
    part = lax.dot_general(
        h_in[:, :width].astype(bf16),
        a_panels[...],
        (((1,), (1,)), ((), ())),
        preferred_element_type=f32,
    )
    r_part[...] = part * h_in[:, width:]
    r_cp = {}
    for d in range(1, mps):
        r_cp[d] = pltpu.make_async_remote_copy(
            src_ref=r_part,
            dst_ref=r_all.at[mp],
            send_sem=r_ss.at[d - 1],
            recv_sem=r_rs.at[d - 1],
            device_id=(rep, me, lax.rem(mp + d, mps)),
            device_id_type=MESH,
        )
        r_cp[d].start()
    r_all[mp] = r_part[...]

    @pl.loop(0, per_group)
    def _(r):
        for j in range(pages):
            rows[r, :, pl.ds(j * page, page), :] = pool[:, page_table[r * pages + j]]

    for d in range(1, mps):
        r_cp[d].wait_recv()
    total = r_all[0]
    for j in range(1, mps):
        total = total + r_all[j]
    for d in range(1, groups):
        f_cp[d].wait_recv()
    delta = jnp.dot(total.astype(bf16), b_panels[...], preferred_element_type=f32)
    q_done = f_all[...].astype(f32) + delta.reshape(groups, block, width)
    q_send[...] = q_done.astype(bf16)
    q_cp = copies(lambda d: q_send.at[peer(d)], q_all.at[me], q_ss, q_rs)
    for d in order:
        q_cp[d].start()
    q_all[me] = q_send[me]

    for d in range(1, groups):
        m_cp[d].wait_recv()
    local = pltpu.make_async_copy(meta_all, meta_s, l_sem)
    local.start()
    local.wait()
    entry_slot = [jnp.int32(r) for r in range(per_group)]
    entry_len = [cached_len[r] for r in range(per_group)]
    source = [jnp.int32(r) for r in range(per_group)]
    for d in range(1, groups):
        origin = lax.rem(me + groups - d, groups)
        count = jnp.int32(0)
        slots = [jnp.int32(0)] * move_cap
        for r in range(per_group):
            hit = meta_s[origin, 0, r] == me
            for k in range(move_cap):
                slots[k] = jnp.where(hit & (count == k), r, slots[k])
            source[r] = jnp.where(
                hit,
                per_group + (d - 1) * move_cap + jnp.minimum(count, move_cap - 1),
                source[r],
            )
            count = count + hit.astype(jnp.int32)
        for k in range(move_cap):
            entry_slot.append(slots[k])
            entry_len.append(meta_s[origin, 1, slots[k]])

    for d in range(1, groups):
        q_cp[d].wait_recv()
    q_in = q_all[...].astype(f32).reshape(sent_rows, width)
    qr = per_kv * steps
    ri = lax.broadcasted_iota(jnp.int32, (qr, per_kv * sent_rows), 0)
    ci = lax.broadcasted_iota(jnp.int32, (qr, per_kv * sent_rows), 1)
    base = ci - (ri // steps) * sent_rows - lax.rem(ri, steps)
    place = jnp.concatenate(
        [(base == targets[r]).astype(f32) for r in range(per_group)], axis=0
    ).astype(bf16)
    for h in range(kv_heads):
        stack = jnp.concatenate(
            [
                q_in[:, (h * per_kv + i) * HEAD : (h * per_kv + i + 1) * HEAD]
                for i in range(per_kv)
            ],
            axis=0,
        ).astype(bf16)
        got = jnp.dot(place, stack, preferred_element_type=f32)
        q_rows[:, h] = got.reshape(per_group, qr, HEAD).astype(bf16)

    scale = HEAD ** (-0.5)
    step_of = lax.rem(lax.broadcasted_iota(jnp.int32, (qr, 1), 0), steps)
    position = lax.broadcasted_iota(jnp.int32, (qr, context), 1)

    def attend(entry, slot, length):
        new = fresh[slot].astype(f32)
        for h in range(kv_heads):
            cols = slice(h * HEAD, (h + 1) * HEAD)
            q = q_rows[slot, h]
            keys = rows[entry, 0, :, cols]
            values = rows[entry, 1, :, cols]
            s = (
                lax.dot_general(
                    q, keys, (((1,), (1,)), ((), ())), preferred_element_type=f32
                )
                * scale
            )
            s = jnp.where(position < length, s, NEG_FILL)
            top = jnp.max(s, axis=1, keepdims=True)
            qf = q.astype(f32)
            extra = []
            for t in range(steps):
                e = jnp.sum(qf * new[2 * t : 2 * t + 1, cols], axis=1, keepdims=True) * scale
                e = jnp.where(step_of >= t, e, NEG_FILL)
                extra.append(e)
                top = jnp.maximum(top, e)
            w = jnp.exp(s - top)
            norm = jnp.sum(w, axis=1, keepdims=True)
            extra = [jnp.exp(e - top) for e in extra]
            for e in extra:
                norm = norm + e
            prob = (w / norm).astype(bf16)
            o = jnp.dot(prob, values, preferred_element_type=f32)
            for t in range(steps):
                pe = (extra[t] / norm).astype(bf16).astype(f32)
                o = o + pe * new[2 * t + 1 : 2 * t + 2, cols]
            att[entry, h] = o.astype(bf16)

    for r in range(per_group):
        attend(r, r, entry_len[r])
    near = sorted(range(1, groups), key=lambda d: min(d, groups - d))
    for k in range(move_cap):
        for d in near:
            slot = (d - 1) * move_cap + k
            p_cp[slot].wait_recv()
            attend(
                per_group + slot, entry_slot[per_group + slot], entry_len[per_group + slot]
            )

    for r in range(per_group):
        cache_out[:, r] = rows[source[r]]
    pr = lax.broadcasted_iota(jnp.int32, (per_kv * own_rows, per_group * qr), 0)
    pc = lax.broadcasted_iota(jnp.int32, (per_kv * own_rows, per_group * qr), 1)
    in_row = lax.rem(pr, own_rows)
    spread = (
        pc == (in_row // steps) * qr + (pr // own_rows) * steps + lax.rem(in_row, steps)
    )
    spread = spread.astype(f32).astype(bf16)
    for h in range(kv_heads):
        stack = jnp.concatenate([att[source[r], h] for r in range(per_group)], axis=0)
        got = jnp.dot(spread, stack, preferred_element_type=f32).astype(bf16)
        for i in range(per_kv):
            att_out[:, (h * per_kv + i) * HEAD : (h * per_kv + i + 1) * HEAD] = got[
                i * own_rows : (i + 1) * own_rows
            ]

    for d in range(1, groups):
        h_cp[d].wait_send()
        f_cp[d].wait_send()
        m_cp[d].wait_send()
        q_cp[d].wait_send()
    for d in range(1, mps):
        r_cp[d].wait_send()
    for slot in p_cp:
        p_cp[slot].wait_send()


def per_device(
    hidden_in,
    frozen_query_rows,
    new_kv,
    adapter_of,
    adapter_home,
    a_store,
    b_store,
    kv_pool,
    page_table,
    cached_len,
    new_group,
):
    groups = lax.axis_size("req")
    mps = lax.axis_size("mp")
    per_group, steps, width = hidden_in.shape
    store_count, rank, _ = a_store.shape
    pages, page = page_table.shape[1], kv_pool.shape[2]
    kv_width = kv_pool.shape[3]
    context = pages * page
    move_cap = -(-(per_group - per_group // 4) // groups)
    cap = -(-per_group // min(16, groups))
    block = -(-cap * steps // 8) * 8
    lanes = store_count * rank
    qr = width // kv_width * steps
    kv_heads = kv_width // HEAD
    moved = (groups - 1) * move_cap
    entries = per_group + moved
    bf16, f32 = jnp.bfloat16, jnp.float32
    cfg = (groups, mps, per_group, steps, cap, block, store_count, rank, pages, page, move_cap)
    dma = pltpu.SemaphoreType.DMA
    att, cache = pl.pallas_call(
        functools.partial(kernel, cfg),
        out_shape=(
            jax.ShapeDtypeStruct((per_group * steps, width), bf16),
            jax.ShapeDtypeStruct((2, per_group, context, kv_width), bf16),
        ),
        in_specs=[pl.BlockSpec(memory_space=SMEM)] * 5 + [pl.BlockSpec(memory_space=VMEM)] * 6,
        out_specs=[pl.BlockSpec(memory_space=VMEM)] * 2,
        scratch_shapes=[
            VMEM((groups, block, width + lanes), bf16),
            VMEM((groups, block, width + lanes), bf16),
            VMEM((groups, block, width), bf16),
            VMEM((groups, block, width), bf16),
            VMEM((groups * block, lanes), f32),
            VMEM((mps, groups * block, lanes), f32),
            VMEM((groups, block, width), bf16),
            VMEM((groups, block, width), bf16),
            VMEM((per_group, kv_heads, qr, HEAD), bf16),
            VMEM((8, 128), jnp.int32),
            VMEM((groups, 8, 128), jnp.int32),
            SMEM((groups, 8, 128), jnp.int32),
            VMEM((moved, 2, context, kv_width), bf16),
            VMEM((entries, 2, context, kv_width), bf16),
            VMEM((entries, kv_heads, qr, HEAD), bf16),
            dma((groups - 1,)),
            dma((groups - 1,)),
            dma((groups - 1,)),
            dma((groups - 1,)),
            dma((mps - 1,)),
            dma((mps - 1,)),
            dma((groups - 1,)),
            dma((groups - 1,)),
            dma((groups - 1,)),
            dma((groups - 1,)),
            dma((moved,)),
            dma((moved,)),
            dma,
        ],
        compiler_params=pltpu.CompilerParams(
            collective_id=0, has_side_effects=True, vmem_limit_bytes=48 * 2**20
        ),
    )(
        adapter_of,
        adapter_home,
        page_table.reshape(-1),
        cached_len,
        new_group,
        hidden_in.reshape(per_group * steps, width),
        frozen_query_rows.reshape(per_group * steps, width),
        new_kv.reshape(per_group, steps * 2, kv_width),
        a_store.reshape(lanes, width),
        b_store.reshape(lanes, width),
        kv_pool,
    )
    return att.reshape(per_group, steps, width), cache


def solution(mesh):
    placed = (
        P(("rep", "req"), None, "mp"),
        P(("rep", "req"), None, "mp"),
        P(("rep", "req"), None, None, "mp"),
        P(("rep", "req")),
        P("rep"),
        P(("rep", "req"), None, "mp"),
        P(("rep", "req"), None, "mp"),
        P(None, ("rep", "req"), None, "mp"),
        P(("rep", "req"), None),
        P(("rep", "req")),
        P(("rep", "req")),
    )
    return jax.shard_map(
        per_device,
        mesh=mesh,
        in_specs=placed,
        out_specs=(P(("rep", "req"), None, "mp"), P(None, ("rep", "req"), None, "mp")),
        check_vma=False,
    )
```

time: 157 us -> 80.6 us (0.51)
  Pallas kernels: 0 us -> 67.6 us
  waiting for transfers between devices: 43.7 us -> 0 us
  local copies, waits for them, and re-layouts: 39.6 us -> 11.9 us
  starting transfers between devices: 27.6 us -> 0 us
  other arithmetic: 24.5 us -> 0 us
  blocking collectives: 10.2 us -> 0 us
  matrix products: 9.32 us -> 0 us
    pallas_call x0 -> x1, Pallas kernels: none -> 67.6 us  [per_device(): pl.pallas_call(functools.partial(kernel, cfg), out_shape=(jax.ShapeDtypeS...]
    all_to_all x6 -> x0, waiting for transfers between devices: 43.7 us -> none  [the longest x1 23.4 us: per_device(): lax.all_to_all(jnp.take(a_store, wanted_slot, axis=0), 'req', split_axis=...]
    all_to_all x6 -> x0, starting transfers between devices: 27.6 us -> none  [the longest x1 6.32 us: per_device(): lax.all_to_all(wanted, 'req', split_axis=0, concat_axis=0, tiled=True)]
    gather x12 -> x0, local copies, waits for them, and re-layouts: 27.1 us -> none  [the longest x2 5.1 us: per_device(): page_rows = jnp.take(kv_pool, page_table.reshape(-1), axis=1)]
    select_n x13 -> x0, other arithmetic: 13.1 us -> none  [the longest x1 2.85 us: per_device(): far_cache = jnp.take(cache_old, safe_src, axis=1)]
    psum x1 -> x0, blocking collectives: 10.2 us -> none  [adapter_rank_width(): return lax.psum(rank_partial_sum, 'mp')]
    dot_general x6 -> x0, matrix products: 9.32 us -> none  [the longest x1 3.48 us: per_device(): jnp.einsum('rsd,rkd->rsk', hidden_in, a_rows, preferred_element_type=jnp....]
    unnamed x28 -> x16, local copies, waits for them, and re-layouts: 2.64 us -> 8.36 us
  transfers between devices with their start and end apart: 6 -> 0, of which waited for: 5 -> 0; matrix products, arithmetic and copies ran while one was open for 31% -> 0% of each run, Pallas kernels for 0% -> 0%
where the time goes in v1:
time: 80.6 us; the launch traced here: 80.2 us
  Pallas kernels  67.6 us (84%)
  local copies, waits for them, and re-layouts  11.9 us (15%)
    pallas_call x1, Pallas kernels, per_device(): pl.pallas_call(functools.partial(kernel, cfg), out_shape=(jax.ShapeDtypeS...  67.6 us
    unnamed x16, local copies, waits for them, and re-layouts  8.36 us

profile of v1, /device:TPU:0, one launch (start us, length us, event | category | flops | bytes accessed | tf_op | source)
XLA Modules:
  0.0 80.2 jit_solution(17109753799269021142)
XLA Ops:
  0.6 0.8 copy.14
  1.4 0.1 reshape.25.page_table
  1.5 0.8 reshape.28.fresh
  2.3 1.0 %reshape.26.hidden = bf16[32,2048]{1,0:T(8,128)(2,1)S(1)} reshape(bf16[16,2,2048]{2,1,0:T(2,128)(2,1)} %param.11) | data formatting | bytes 262144 | tf_op jit(solution)/shard_map/reshape | solution.py:425
  3.2 1.0 %reshape.27.frozen = bf16[32,2048]{1,0:T(8,128)(2,1)S(1)} reshape(bf16[16,2,2048]{2,1,0:T(2,128)(2,1)} %param.12) | data formatting | bytes 262144 | tf_op jit(solution)/shard_map/reshape | solution.py:426
  4.2 0.0 copy-start
  4.2 1.6 %copy-done = bf16[2,128,16,256]{3,2,1,0:T(8,128)(2,1)S(1)} copy-done((bf16[2,128,16,256]{3,2,1,0:T(8,128)(2,1)S(1)}, bf16[2,128,16,256]{3,2,1,0:T(8,128)(2,1)}, u32[]{:S(2)}) %copy-start) | copy-done | bytes 2097176
  5.8 0.0 copy-start.1
  5.8 1.0 %copy-done.1 = bf16[2,64,2048]{2,1,0:T(8,128)(2,1)S(1)} copy-done((bf16[2,64,2048]{2,1,0:T(8,128)(2,1)S(1)}, bf16[2,64,2048]{2,1,0:T(8,128)(2,1)}, u32[]{:S(2)}) %copy-start.1) | copy-done | bytes 524312
  6.8 0.0 copy-start.2
  6.8 1.0 %copy-done.2 = bf16[2,64,2048]{2,1,0:T(8,128)(2,1)S(1)} copy-done((bf16[2,64,2048]{2,1,0:T(8,128)(2,1)S(1)}, bf16[2,64,2048]{2,1,0:T(8,128)(2,1)}, u32[]{:S(2)}) %copy-start.2) | copy-done | bytes 524312
  7.9 0.0 copy-start.3
  7.9 0.7 copy-done.3
  8.5 0.0 copy-start.4
  8.5 0.7 copy-done.4
  9.2 0.0 copy-start.5
  9.2 0.7 copy-done.5
  9.8 0.0 copy-start.6
  9.8 0.7 copy-done.6
  10.5 67.6 %shard_map.122 = (bf16[32,2048]{1,0:T(8,128)(2,1)S(1)}, bf16[2,16,128,256]{3,2,1,0:T(8,128)(2,1)S(1)}) custom-call(s32[16]{0:T(128)S(1)} %copy-done.3, s32[8]{0:T(128)S(1)} %copy-done.4, s32[128]{0:T(128)S(1)} %reshape.25.page_table, s32[16]{0:T(128)S(1)} %copy-done.5, s32[16]{0:T(128)S(1)} %copy-done.6, bf16[32,2048]{1,0:T(8,128)(2,1)S(1)} %reshape.26.hidden, ...), custom_call_target="tpu_custom_call" | custom-call | tf_op jit(solution)/shard_map/pallas_call | solution.py:378
  78.1 0.8 reshape.31
  78.9 1.3 %copy.16 = bf16[2,16,128,256]{3,2,1,0:T(8,128)(2,1)} copy(bf16[2,16,128,256]{3,2,1,0:T(8,128)(2,1)S(1)} %get-tuple-element.9) | data formatting | bytes 4194304
Async XLA Ops:
  4.2 1.6 %copy-start = (bf16[2,128,16,256]{3,2,1,0:T(8,128)(2,1)S(1)}, bf16[2,128,16,256]{3,2,1,0:T(8,128)(2,1)}, u32[]{:S(2)}) copy-start(bf16[2,128,16,256]{3,2,1,0:T(8,128)(2,1)} %pool.1) | copy-start | bytes 6291460
  5.8 1.0 %copy-start.1 = (bf16[2,64,2048]{2,1,0:T(8,128)(2,1)S(1)}, bf16[2,64,2048]{2,1,0:T(8,128)(2,1)}, u32[]{:S(2)}) copy-start(bf16[2,64,2048]{2,1,0:T(8,128)(2,1)} %param.16) | copy-start | bytes 1572868
  6.8 1.0 %copy-start.2 = (bf16[2,64,2048]{2,1,0:T(8,128)(2,1)S(1)}, bf16[2,64,2048]{2,1,0:T(8,128)(2,1)}, u32[]{:S(2)}) copy-start(bf16[2,64,2048]{2,1,0:T(8,128)(2,1)} %param.17) | copy-start | bytes 1572868
  7.9 0.7 copy-start.3
  8.5 0.7 copy-start.4
  9.2 0.7 copy-start.5
  9.8 0.7 copy-start.6

commit v2 on v1

--- a/solution.py
+++ b/solution.py
@@ -16,17 +16,17 @@
 
 def kernel(
     cfg,
-    adapter_of,
-    adapter_home,
-    page_table,
-    cached_len,
-    new_group,
-    hidden,
-    frozen,
-    fresh,
-    a_panels,
-    b_panels,
-    pool,
+    *refs,
+):
+    given, refs = refs[:11], refs[11:]
+    body(cfg, given, refs[2:13], refs[13], *refs[:2], *refs[14:])
+
+
+def body(
+    cfg,
+    given,
+    held,
+    in_sem,
     att_out,
     cache_out,
     h_send,
@@ -38,6 +38,7 @@
     q_send,
     q_all,
     q_rows,
+    wide,
     meta_send,
     meta_all,
     meta_s,
@@ -63,7 +64,26 @@
     rep = lax.axis_index("rep")
     me = lax.axis_index("req")
     mp = lax.axis_index("mp")
-    width = hidden.shape[1]
+    fetch = [
+        pltpu.make_async_copy(src, dst, in_sem.at[i])
+        for i, (src, dst) in enumerate(zip(given, held))
+    ]
+    for f in fetch:
+        f.start()
+    (
+        adapter_of,
+        adapter_home,
+        page_table,
+        cached_len,
+        new_group,
+        hidden,
+        frozen,
+        fresh,
+        pool,
+        a_panels,
+        b_panels,
+    ) = held
+    width = hidden.shape[2]
     lanes = store_count * rank
     kv_width = pool.shape[3]
     kv_heads = kv_width // HEAD
@@ -85,6 +105,9 @@
         pl.semaphore_signal(
             barrier, inc=1, device_id=(rep, me, lax.rem(mp + d, mps)), device_id_type=MESH
         )
+
+    for f in fetch[:6]:
+        f.wait()
 
     owners, picks, targets = [], [], []
     for r in range(per_group):
@@ -108,7 +131,12 @@
     pick_by_owner = (row == want).astype(f32).astype(bf16)
     mask = (mlane == mpick).astype(f32).astype(bf16)
 
-    h_out = jnp.dot(pick_by_owner, hidden[...], preferred_element_type=f32)
+    def flat(ref):
+        for r in range(per_group):
+            wide[r * steps : (r + 1) * steps] = ref[r].astype(f32)
+        return wide[...].astype(bf16)
+
+    h_out = jnp.dot(pick_by_owner, flat(hidden), preferred_element_type=f32)
     m_out = jnp.dot(pick_by_owner, mask, preferred_element_type=f32)
     h_send[:, :, :width] = h_out.reshape(groups, block, width).astype(bf16)
     h_send[:, :, width:] = m_out.reshape(groups, block, lanes).astype(bf16)
@@ -141,7 +169,8 @@
         h_cp[d].start()
     h_all[me] = h_send[me]
 
-    f_out = jnp.dot(pick_by_owner, frozen[...], preferred_element_type=f32)
+    fetch[6].wait()
+    f_out = jnp.dot(pick_by_owner, flat(frozen), preferred_element_type=f32)
     f_send[...] = f_out.reshape(groups, block, width).astype(bf16)
     f_cp = copies(lambda d: f_send.at[peer(d)], f_all.at[me], f_ss, f_rs)
     for d in order:
@@ -152,6 +181,7 @@
         m_cp[d].start()
     meta_all[me] = meta
 
+    fetch[8].wait()
     p_cp = {}
     for d in order:
         dest = peer(d)
@@ -165,7 +195,7 @@
         for k in range(move_cap):
             slot = (d - 1) * move_cap + k
             for j in range(pages):
-                page_id = page_table[sources[k] * pages + j]
+                page_id = page_table[sources[k], j]
                 page_send[slot, :, pl.ds(j * page, page), :] = pool[:, page_id]
             p_cp[slot] = pltpu.make_async_remote_copy(
                 src_ref=page_send.at[slot],
@@ -175,8 +205,14 @@
                 device_id=send_to(d),
                 device_id_type=MESH,
             )
-            p_cp[slot].start()
-
+
+    def send_pages(k):
+        for d in order:
+            p_cp[(d - 1) * move_cap + k].start()
+
+    send_pages(0)
+
+    fetch[9].wait()
     for d in range(1, groups):
         h_cp[d].wait_recv()
     h_in = h_all[...].astype(f32).reshape(sent_rows, width + lanes)
@@ -203,13 +239,14 @@
     @pl.loop(0, per_group)
     def _(r):
         for j in range(pages):
-            rows[r, :, pl.ds(j * page, page), :] = pool[:, page_table[r * pages + j]]
+            rows[r, :, pl.ds(j * page, page), :] = pool[:, page_table[r, j]]
 
     for d in range(1, mps):
         r_cp[d].wait_recv()
     total = r_all[0]
     for j in range(1, mps):
         total = total + r_all[j]
+    fetch[10].wait()
     for d in range(1, groups):
         f_cp[d].wait_recv()
     delta = jnp.dot(total.astype(bf16), b_panels[...], preferred_element_type=f32)
@@ -218,7 +255,10 @@
     q_cp = copies(lambda d: q_send.at[peer(d)], q_all.at[me], q_ss, q_rs)
     for d in order:
         q_cp[d].start()
+    for k in range(1, move_cap):
+        send_pages(k)
     q_all[me] = q_send[me]
+    fetch[7].wait()
 
     for d in range(1, groups):
         m_cp[d].wait_recv()
@@ -268,53 +308,59 @@
         q_rows[:, h] = got.reshape(per_group, qr, HEAD).astype(bf16)
 
     scale = HEAD ** (-0.5)
-    step_of = lax.rem(lax.broadcasted_iota(jnp.int32, (qr, 1), 0), steps)
     position = lax.broadcasted_iota(jnp.int32, (qr, context), 1)
 
-    def attend(entry, slot, length):
-        new = fresh[slot].astype(f32)
-        for h in range(kv_heads):
-            cols = slice(h * HEAD, (h + 1) * HEAD)
-            q = q_rows[slot, h]
-            keys = rows[entry, 0, :, cols]
-            values = rows[entry, 1, :, cols]
-            s = (
-                lax.dot_general(
-                    q, keys, (((1,), (1,)), ((), ())), preferred_element_type=f32
+    def attend(items):
+        work = []
+        for entry, slot, length in items:
+            new = [fresh[slot, t].astype(f32) for t in range(steps)]
+            for h in range(kv_heads):
+                cols = slice(h * HEAD, (h + 1) * HEAD)
+                q = q_rows[slot, h]
+                s = lax.dot_general(
+                    q, rows[entry, 0, :, cols], (((1,), (1,)), ((), ())), preferred_element_type=f32
                 )
-                * scale
-            )
-            s = jnp.where(position < length, s, NEG_FILL)
-            top = jnp.max(s, axis=1, keepdims=True)
-            qf = q.astype(f32)
-            extra = []
+                s = jnp.where(position < length, s * scale, NEG_FILL)
+                qf = q.astype(f32)
+                extra = [
+                    jnp.sum(qf * new[t][0:1, cols], axis=1, keepdims=True)
+                    for t in range(steps)
+                ]
+                work.append((entry, h, cols, new, s, extra))
+        scores = jnp.concatenate([w[4] for w in work], axis=0)
+        extra = [jnp.concatenate([w[5][t] for w in work], axis=0) * scale for t in range(steps)]
+        step_of = lax.rem(
+            lax.broadcasted_iota(jnp.int32, (len(work) * qr, 1), 0), steps
+        )
+        extra = [jnp.where(step_of >= t, extra[t], NEG_FILL) for t in range(steps)]
+        top = jnp.max(scores, axis=1, keepdims=True)
+        for e in extra:
+            top = jnp.maximum(top, e)
+        weights = jnp.exp(scores - top)
+        extra = [jnp.exp(e - top) for e in extra]
+        norm = jnp.sum(weights, axis=1, keepdims=True)
+        for e in extra:
+            norm = norm + e
+        prob = (weights / norm).astype(bf16)
+        extra = [(e / norm).astype(bf16).astype(f32) for e in extra]
+        for n, (entry, h, cols, new, _, _) in enumerate(work):
+            part = slice(n * qr, (n + 1) * qr)
+            o = jnp.dot(prob[part], rows[entry, 1, :, cols], preferred_element_type=f32)
             for t in range(steps):
-                e = jnp.sum(qf * new[2 * t : 2 * t + 1, cols], axis=1, keepdims=True) * scale
-                e = jnp.where(step_of >= t, e, NEG_FILL)
-                extra.append(e)
-                top = jnp.maximum(top, e)
-            w = jnp.exp(s - top)
-            norm = jnp.sum(w, axis=1, keepdims=True)
-            extra = [jnp.exp(e - top) for e in extra]
-            for e in extra:
-                norm = norm + e
-            prob = (w / norm).astype(bf16)
-            o = jnp.dot(prob, values, preferred_element_type=f32)
-            for t in range(steps):
-                pe = (extra[t] / norm).astype(bf16).astype(f32)
-                o = o + pe * new[2 * t + 1 : 2 * t + 2, cols]
+                o = o + extra[t][part] * new[t][1:2, cols]
             att[entry, h] = o.astype(bf16)
 
-    for r in range(per_group):
-        attend(r, r, entry_len[r])
+    for r in range(0, per_group, 4):
+        attend([(e, e, entry_len[e]) for e in range(r, min(r + 4, per_group))])
     near = sorted(range(1, groups), key=lambda d: min(d, groups - d))
     for k in range(move_cap):
-        for d in near:
-            slot = (d - 1) * move_cap + k
-            p_cp[slot].wait_recv()
-            attend(
-                per_group + slot, entry_slot[per_group + slot], entry_len[per_group + slot]
-            )
+        for n in range(0, len(near), 3):
+            items = []
+            for d in near[n : n + 3]:
+                p_cp[(d - 1) * move_cap + k].wait_recv()
+                e = per_group + (d - 1) * move_cap + k
+                items.append((e, entry_slot[e], entry_len[e]))
+            attend(items)
 
     for r in range(per_group):
         cache_out[:, r] = rows[source[r]]
@@ -375,15 +421,31 @@
     bf16, f32 = jnp.bfloat16, jnp.float32
     cfg = (groups, mps, per_group, steps, cap, block, store_count, rank, pages, page, move_cap)
     dma = pltpu.SemaphoreType.DMA
+    given = (
+        adapter_of,
+        adapter_home,
+        page_table,
+        cached_len,
+        new_group,
+        hidden_in,
+        frozen_query_rows,
+        new_kv,
+        kv_pool,
+        a_store.reshape(lanes, width),
+        b_store.reshape(lanes, width),
+    )
     att, cache = pl.pallas_call(
         functools.partial(kernel, cfg),
         out_shape=(
             jax.ShapeDtypeStruct((per_group * steps, width), bf16),
             jax.ShapeDtypeStruct((2, per_group, context, kv_width), bf16),
         ),
-        in_specs=[pl.BlockSpec(memory_space=SMEM)] * 5 + [pl.BlockSpec(memory_space=VMEM)] * 6,
+        in_specs=[pl.BlockSpec(memory_space=pltpu.HBM)] * len(given),
         out_specs=[pl.BlockSpec(memory_space=VMEM)] * 2,
-        scratch_shapes=[
+        scratch_shapes=[SMEM(g.shape, g.dtype) for g in given[:5]]
+        + [VMEM(g.shape, g.dtype) for g in given[5:]]
+        + [
+            dma((len(given),)),
             VMEM((groups, block, width + lanes), bf16),
             VMEM((groups, block, width + lanes), bf16),
             VMEM((groups, block, width), bf16),
@@ -393,6 +455,7 @@
             VMEM((groups, block, width), bf16),
             VMEM((groups, block, width), bf16),
             VMEM((per_group, kv_heads, qr, HEAD), bf16),
+            VMEM((per_group * steps, width), f32),
             VMEM((8, 128), jnp.int32),
             VMEM((groups, 8, 128), jnp.int32),
             SMEM((groups, 8, 128), jnp.int32),
@@ -414,21 +477,9 @@
             dma,
         ],
         compiler_params=pltpu.CompilerParams(
-            collective_id=0, has_side_effects=True, vmem_limit_bytes=48 * 2**20
+            collective_id=0, has_side_effects=True, vmem_limit_bytes=62 * 2**20
         ),
-    )(
-        adapter_of,
-        adapter_home,
-        page_table.reshape(-1),
-        cached_len,
-        new_group,
-        hidden_in.reshape(per_group * steps, width),
-        frozen_query_rows.reshape(per_group * steps, width),
-        new_kv.reshape(per_group, steps * 2, kv_width),
-        a_store.reshape(lanes, width),
-        b_store.reshape(lanes, width),
-        kv_pool,
-    )
+    )(*given)
     return att.reshape(per_group, steps, width), cache
 
 

time: 80.6 us -> 57 us (0.71)
  Pallas kernels: 67.6 us -> 50 us
  local copies, waits for them, and re-layouts: 11.9 us -> 6.15 us
    pallas_call x1, Pallas kernels: 67.6 us -> 50 us  [per_device(): pl.pallas_call(functools.partial(kernel, cfg), out_shape=(jax.ShapeDtypeS...]
    unnamed x16 -> x2, local copies, waits for them, and re-layouts: 8.36 us -> 4.48 us
    reshape x4 -> x0, local copies, waits for them, and re-layouts: 2.79 us -> none  [the longest x1 0.96 us: per_device(): frozen_query_rows.reshape(per_group * steps, width)]
    reshape x1, local copies, waits for them, and re-layouts: 0.76 us -> 1.66 us  [per_device(): return (att.reshape(per_group, steps, width), cache)]
where the time goes in v2:
time: 57 us; the launch traced here: 56.8 us
  Pallas kernels  50 us (88%)
  local copies, waits for them, and re-layouts  6.15 us (11%)
  between operations  0.64 us (1%)
    pallas_call x1, Pallas kernels, per_device(): pl.pallas_call(functools.partial(kernel, cfg), out_shape=(jax.ShapeDtypeS...  50 us
    unnamed x2, local copies, waits for them, and re-layouts  4.48 us
    reshape x1, local copies, waits for them, and re-layouts, per_device(): return (att.reshape(per_group, steps, width), cache)  1.66 us

profile of v2, /device:TPU:0, one launch (start us, length us, event | category | flops | bytes accessed | tf_op | source)
XLA Modules:
  0.0 56.8 jit_solution(5304429906288046538)
XLA Ops:
  0.6 1.4 %copy.13.refs_2_ = s32[16,8]{1,0:T(8,128)} copy(s32[16,8]{0,1:T(8,128)} %param.19) | data formatting | bytes 1024 | tf_op args[8]
  2.0 50.0 %shard_map.122 = (bf16[32,2048]{1,0:T(8,128)(2,1)}, bf16[2,16,128,256]{3,2,1,0:T(8,128)(2,1)}) custom-call(s32[16]{0:T(128)} %refs_0_.1, s32[8]{0:T(128)} %refs_1_.1, s32[16,8]{1,0:T(8,128)} %copy.13.refs_2_, s32[16]{0:T(128)} %refs_3_.1, s32[16]{0:T(128)} %refs_4_.1, bf16[16,2,2048]{2,1,0:T(2,128)(2,1)} %refs_5_.1, bf16[16,2,2048]{2,1,0:T(2,128)(2,1)} %refs_6_.1, ...), custom_call_target="tpu_custom_call" | custom-call | tf_op jit(solution)/shard_map/pallas_call | solution.py:437
  52.0 1.7 %reshape.15 = bf16[16,2,2048]{2,1,0:T(2,128)(2,1)} reshape(bf16[32,2048]{1,0:T(8,128)(2,1)} %get-tuple-element.4) | data formatting | bytes 262144 | tf_op jit(solution)/shard_map/reshape | solution.py:483
  53.6 3.1 %copy.15 = bf16[2,16,128,256]{3,2,1,0:T(8,128)(2,1)} copy(bf16[2,16,128,256]{3,2,1,0:T(8,128)(2,1)} %get-tuple-element.9) | data formatting | bytes 4194304

commit v3 on v2

--- a/solution.py
+++ b/solution.py
@@ -195,7 +195,7 @@
         for k in range(move_cap):
             slot = (d - 1) * move_cap + k
             for j in range(pages):
-                page_id = page_table[sources[k], j]
+                page_id = page_table[j, sources[k]]
                 page_send[slot, :, pl.ds(j * page, page), :] = pool[:, page_id]
             p_cp[slot] = pltpu.make_async_remote_copy(
                 src_ref=page_send.at[slot],
@@ -239,7 +239,7 @@
     @pl.loop(0, per_group)
     def _(r):
         for j in range(pages):
-            rows[r, :, pl.ds(j * page, page), :] = pool[:, page_table[r, j]]
+            rows[r, :, pl.ds(j * page, page), :] = pool[:, page_table[j, r]]
 
     for d in range(1, mps):
         r_cp[d].wait_recv()
@@ -424,7 +424,7 @@
     given = (
         adapter_of,
         adapter_home,
-        page_table,
+        page_table.T,
         cached_len,
         new_group,
         hidden_in,
@@ -477,9 +477,9 @@
             dma,
         ],
         compiler_params=pltpu.CompilerParams(
-            collective_id=0, has_side_effects=True, vmem_limit_bytes=62 * 2**20
+            collective_id=0, has_side_effects=True, vmem_limit_bytes=40 * 2**20
         ),
-    )(*given)
+    )(*[pltpu.with_memory_space_constraint(g, pltpu.HBM) for g in given])
     return att.reshape(per_group, steps, width), cache
 
 

time: 57 us -> 51.5 us (0.904)
  local copies, waits for them, and re-layouts: 6.15 us -> 2.08 us
  Pallas kernels: 50 us -> 48.6 us
    unnamed x2 -> x1, local copies, waits for them, and re-layouts: 4.48 us -> 1.32 us
    pallas_call x1, Pallas kernels: 50 us -> 48.6 us  [per_device(): pl.pallas_call(functools.partial(kernel, cfg), out_shape=(jax.ShapeDtypeS...]
    reshape x1, local copies, waits for them, and re-layouts: 1.66 us -> 0.76 us  [per_device(): return (att.reshape(per_group, steps, width), cache)]
where the time goes in v3:
time: 51.5 us; the launch traced here: 51.3 us
  Pallas kernels  48.6 us (94%)
  local copies, waits for them, and re-layouts  2.08 us (4%)
  between operations  0.64 us (1%)
    pallas_call x1, Pallas kernels, per_device(): pl.pallas_call(functools.partial(kernel, cfg), out_shape=(jax.ShapeDtypeS...  48.6 us
    unnamed x1, local copies, waits for them, and re-layouts  1.32 us

profile of v3, /device:TPU:0, one launch (start us, length us, event | category | flops | bytes accessed | tf_op | source)
XLA Modules:
  0.0 51.3 jit_solution(14629471596791807215)
XLA Ops:
  0.6 48.6 %shard_map.122 = (bf16[32,2048]{1,0:T(8,128)(2,1)S(1)}, bf16[2,16,128,256]{3,2,1,0:T(8,128)(2,1)S(1)}) custom-call(s32[16]{0:T(128)} %refs_0_.1, s32[8]{0:T(128)} %refs_1_.1, s32[8,16]{1,0:T(8,128)} %bitcast.5, s32[16]{0:T(128)} %refs_3_.1, s32[16]{0:T(128)} %refs_4_.1, bf16[16,2,2048]{2,1,0:T(2,128)(2,1)} %refs_5_.1, bf16[16,2,2048]{2,1,0:T(2,128)(2,1)} %refs_6_.1, ...), custom_call_target="tpu_custom_call" | custom-call | tf_op jit(solution)/shard_map/pallas_call | solution.py:437
  49.3 0.8 %reshape.15 = bf16[16,2,2048]{2,1,0:T(2,128)(2,1)} reshape(bf16[32,2048]{1,0:T(8,128)(2,1)S(1)} %get-tuple-element.4) | data formatting | bytes 262144 | tf_op jit(solution)/shard_map/reshape | solution.py:483
  50.0 1.3 %copy.14 = bf16[2,16,128,256]{3,2,1,0:T(8,128)(2,1)} copy(bf16[2,16,128,256]{3,2,1,0:T(8,128)(2,1)S(1)} %get-tuple-element.9) | data formatting | bytes 4194304

commit v4 on v3

--- a/solution.py
+++ b/solution.py
@@ -182,20 +182,23 @@
     meta_all[me] = meta
 
     fetch[8].wait()
-    p_cp = {}
+    p_cp, sources = {}, {}
     for d in order:
         dest = peer(d)
         count = jnp.int32(0)
-        sources = [jnp.int32(0)] * move_cap
+        picked = [jnp.int32(0)] * move_cap
         for r in range(per_group):
             hit = new_group[r] == dest
             for k in range(move_cap):
-                sources[k] = jnp.where(hit & (count == k), r, sources[k])
+                picked[k] = jnp.where(hit & (count == k), r, picked[k])
             count = count + hit.astype(jnp.int32)
-        for k in range(move_cap):
+        sources[d] = picked
+
+    def pack_pages(k):
+        for d in order:
             slot = (d - 1) * move_cap + k
             for j in range(pages):
-                page_id = page_table[j, sources[k]]
+                page_id = page_table[j, sources[d][k]]
                 page_send[slot, :, pl.ds(j * page, page), :] = pool[:, page_id]
             p_cp[slot] = pltpu.make_async_remote_copy(
                 src_ref=page_send.at[slot],
@@ -205,12 +208,14 @@
                 device_id=send_to(d),
                 device_id_type=MESH,
             )
+            if k == 0 or (k == 1 and d == order[0]):
+                p_cp[slot].start()
 
     def send_pages(k):
-        for d in order:
+        for d in order[1:] if k == 1 else order:
             p_cp[(d - 1) * move_cap + k].start()
 
-    send_pages(0)
+    pack_pages(0)
 
     fetch[9].wait()
     for d in range(1, groups):
@@ -235,6 +240,9 @@
         )
         r_cp[d].start()
     r_all[mp] = r_part[...]
+
+    for k in range(1, move_cap):
+        pack_pages(k)
 
     @pl.loop(0, per_group)
     def _(r):

time: 51.5 us -> 51.5 us (level)
  no operation moved by 1% of the time
where the time goes in v4:
time: 51.5 us; the launch traced here: 51.3 us
  Pallas kernels  48.6 us (94%)
  local copies, waits for them, and re-layouts  2.08 us (4%)
  between operations  0.64 us (1%)
    pallas_call x1, Pallas kernels, per_device(): pl.pallas_call(functools.partial(kernel, cfg), out_shape=(jax.ShapeDtypeS...  48.6 us
    unnamed x1, local copies, waits for them, and re-layouts  1.32 us

profile of v4, /device:TPU:0, one launch (start us, length us, event | category | flops | bytes accessed | tf_op | source)
XLA Modules:
  0.0 51.3 jit_solution(6734301335022540595)
XLA Ops:
  0.6 48.6 %shard_map.122 = (bf16[32,2048]{1,0:T(8,128)(2,1)S(1)}, bf16[2,16,128,256]{3,2,1,0:T(8,128)(2,1)S(1)}) custom-call(s32[16]{0:T(128)} %refs_0_.1, s32[8]{0:T(128)} %refs_1_.1, s32[8,16]{1,0:T(8,128)} %bitcast.5, s32[16]{0:T(128)} %refs_3_.1, s32[16]{0:T(128)} %refs_4_.1, bf16[16,2,2048]{2,1,0:T(2,128)(2,1)} %refs_5_.1, bf16[16,2,2048]{2,1,0:T(2,128)(2,1)} %refs_6_.1, ...), custom_call_target="tpu_custom_call" | custom-call | tf_op jit(solution)/shard_map/pallas_call | solution.py:445
  49.2 0.8 %reshape.15 = bf16[16,2,2048]{2,1,0:T(2,128)(2,1)} reshape(bf16[32,2048]{1,0:T(8,128)(2,1)S(1)} %get-tuple-element.4) | data formatting | bytes 262144 | tf_op jit(solution)/shard_map/reshape | solution.py:491
  50.0 1.3 %copy.14 = bf16[2,16,128,256]{3,2,1,0:T(8,128)(2,1)} copy(bf16[2,16,128,256]{3,2,1,0:T(8,128)(2,1)S(1)} %get-tuple-element.9) | data formatting | bytes 4194304
